TPU v7x, 32 devices: a whole 2x2x4 slice. The times are simulated.
32 devices in a mesh: dp: 2 (over x), expert: 16 (over z, y, core).
Axes of the slice: x: 2, y: 2, z: 4, core: 2. Of those that a mesh axis runs over, the one named last changes fastest.
Arguments:
- saved_inputs: bfloat16 [1024, 3584], P('expert'), may hold values from -6 to 6
- output_grad: bfloat16 [1024, 3584], P('expert'), may hold values from -6 to 6
- routes: int32 [1024, 8], P('expert'), may hold values from 0 to 15, all different within a row; in each aligned block of 64 rows (0 to 63, 64 to 127, ...) at most 36 rows name the same one
- route_gates: bfloat16 [1024, 8], P('expert'), may hold values from 0.099609375 to 1
- expert_gate: bfloat16 [16, 3584, 1024], P('expert', None, 'dp'), may hold values from -0.09375 to 0.09375
- expert_up: bfloat16 [16, 3584, 1024], P('expert', None, 'dp'), may hold values from -0.09375 to 0.09375
- expert_down: bfloat16 [16, 1024, 3584], P('expert', 'dp'), may hold values from -0.1875 to 0.1875
- proj_basis: bfloat16 [16, 1024, 128], P('expert', 'dp'), may hold values from -0.1875 to 0.1875
Outputs:
- input_grad: bfloat16 [1024, 3584], P('expert', 'dp')
- projected: float32 [16, 3584, 3, 128], P('expert', 'dp')
Inputs may be any that keep to these rules, and one draw needn't show every extreme that they name: Within each aligned block of 64 tokens no expert is named by more than 36 routes, and in every draw some expert is named by exactly 36.
All inputs are finite; a program needn't handle non-finite values.
Results may differ from a plain program's by a relative error of at most 0.009.
Values may be sent and summed in bfloat16 or wider, within the bound.
A program may use at most 128 MiB of HBM per device.

v0:
```python
import jax
import jax.numpy as jnp
from jax import lax
from jax.sharding import PartitionSpec as P


def on_device(
    saved_inputs, output_grad, routes, route_gates, expert_gate, expert_up, expert_down, proj_basis
):
    token_count, model_width = saved_inputs.shape
    top_count = routes.shape[1]
    expert_count = lax.axis_size("expert")
    group_count = lax.axis_size("dp")
    capacity = token_count * top_count * 9 // (8 * expert_count)
    slot_count = expert_count * capacity
    column_width = model_width // group_count
    route_count = token_count * top_count
    flat_routes = routes.reshape(-1)
    one_hot = (flat_routes[:, None] == jnp.arange(expert_count, dtype=jnp.int32)[None, :]).astype(
        jnp.int32
    )
    earlier = jnp.sum((jnp.cumsum(one_hot, axis=0) - one_hot) * one_hot, axis=1)
    target_slot = flat_routes * capacity + earlier
    slot_owner = (
        jnp.full((slot_count,), route_count, jnp.int32)
        .at[target_slot]
        .set(jnp.arange(route_count, dtype=jnp.int32))
    )
    filled = slot_owner < route_count
    safe_route = jnp.minimum(slot_owner, route_count - 1)
    source_token = safe_route // top_count
    zero_half = jnp.zeros((), jnp.bfloat16)
    gate_slots = jnp.where(filled, route_gates.reshape(-1)[safe_route], zero_half).reshape(
        expert_count, capacity
    )
    token_map = (
        (source_token[None, :] == jnp.arange(token_count, dtype=jnp.int32)[:, None])
        & filled[None, :]
    ).astype(jnp.bfloat16)
    contract_first = (((0,), (0,)), ((), ()))

    def to_slots(source_rows):
        picked = lax.dot_general(
            token_map, source_rows, contract_first, preferred_element_type=jnp.float32
        ).astype(jnp.bfloat16)
        return picked.reshape(expert_count, capacity * source_rows.shape[1])

    recv_inputs, recv_grads, recv_gates = (
        lax.all_to_all(to_slots(saved_inputs), "expert", split_axis=0, concat_axis=0, tiled=True),
        lax.all_to_all(to_slots(output_grad), "expert", split_axis=0, concat_axis=0, tiled=True),
        lax.all_to_all(gate_slots, "expert", split_axis=0, concat_axis=0, tiled=True),
    )
    input_rows = recv_inputs.reshape(slot_count, model_width)
    grad_rows = recv_grads.reshape(slot_count, model_width)
    gain = recv_gates.reshape(slot_count, 1).astype(jnp.float32)
    gate_w = expert_gate[0]
    up_w = expert_up[0]
    down_w = expert_down[0]
    basis = proj_basis[0]
    rank_width = basis.shape[1]
    contract_last = (((1,), (1,)), ((), ()))
    pre_gate = jnp.dot(input_rows, gate_w, preferred_element_type=jnp.float32)
    pre_up = jnp.dot(input_rows, up_w, preferred_element_type=jnp.float32)
    grad_hidden = lax.dot_general(
        grad_rows, down_w, contract_last, preferred_element_type=jnp.float32
    )
    sigma = jax.nn.sigmoid(pre_gate)
    silu_val = pre_gate * sigma
    scaled = gain * grad_hidden
    grad_up = (scaled * silu_val).astype(jnp.bfloat16)
    grad_gate = (scaled * pre_up * sigma * (1.0 + pre_gate * (1.0 - sigma))).astype(jnp.bfloat16)
    hidden = (silu_val * pre_up).astype(jnp.bfloat16)
    part_rows = (
        lax.dot_general(grad_gate, gate_w, contract_last, preferred_element_type=jnp.float32)
        + lax.dot_general(grad_up, up_w, contract_last, preferred_element_type=jnp.float32)
    ).astype(jnp.bfloat16)
    coef_gate = jnp.dot(grad_gate, basis, preferred_element_type=jnp.float32).astype(jnp.bfloat16)
    coef_up = jnp.dot(grad_up, basis, preferred_element_type=jnp.float32).astype(jnp.bfloat16)
    coef_down = (gain * jnp.dot(hidden, basis, preferred_element_type=jnp.float32)).astype(
        jnp.bfloat16
    )
    coef_pair = jnp.concatenate([coef_gate, coef_up], axis=1)
    front = lax.dot_general(
        input_rows, coef_pair, contract_first, preferred_element_type=jnp.float32
    )
    rear = lax.dot_general(grad_rows, coef_down, contract_first, preferred_element_type=jnp.float32)
    summed_terms = lax.psum_scatter(
        jnp.concatenate([front, rear], axis=1).astype(jnp.bfloat16),
        "dp",
        scatter_dimension=0,
        tiled=True,
    ).astype(jnp.float32)
    projected = summed_terms.reshape(1, column_width, 3, rank_width)
    returned = lax.all_to_all(
        part_rows.reshape(expert_count, capacity * model_width),
        "expert",
        split_axis=0,
        concat_axis=0,
        tiled=True,
    )
    spread = jnp.dot(
        token_map, returned.reshape(slot_count, model_width), preferred_element_type=jnp.float32
    )
    token_grad = lax.psum_scatter(
        spread.astype(jnp.bfloat16), "dp", scatter_dimension=1, tiled=True
    )
    return (token_grad, projected)


def solution(mesh):
    placed = (
        P("expert", None),
        P("expert", None),
        P("expert", None),
        P("expert", None),
        P("expert", None, "dp"),
        P("expert", None, "dp"),
        P("expert", "dp", None),
        P("expert", "dp", None),
    )
    return jax.shard_map(
        on_device,
        mesh=mesh,
        in_specs=placed,
        out_specs=(P("expert", "dp"), P("expert", "dp", None, None)),
        check_vma=False,
    )
```

profile of v0, /device:TPU:0, one launch (start us, length us, event | category | flops | bytes accessed | tf_op | source)
XLA Modules:
  0.0 535.6 jit_solution(17826223306023978186)
XLA Ops:
  7.2 0.0 copy-start
  7.2 0.8 copy.28
  8.0 0.1 eq.42
  8.1 0.1 eq.38
  8.2 0.7 broadcast_multiply_fusion
  8.9 1.1 reduce-window.6
  10.0 0.2 slice_reduce_fusion
  10.3 0.1 copy.27
  10.4 0.1 mul.58
  10.5 0.1 fusion.36
  10.6 2.4 scatter_custom_fusion
  13.1 0.8 copy.31
  13.9 0.1 reshape.101
  14.0 3.9 gather_fusion
  17.9 0.7 all_to_all.32
  18.6 7.4 %all-to-all-start = ((bf16[16,1,36]{2,1,0:T(2,128)(2,1)}), bf16[16,1,36]{2,1,0:T(2,128)(2,1)S(1)}, u32[]{:S(2)}, u32[]{:S(2)}) async-start(bf16[16,1,36]{2,1,0:T(2,128)(2,1)} %all_to_all.32), calls=%async_computation | async-start | bytes 16384 | tf_op jit(solution)/shard_map/all_to_all | solution.py:51
  26.1 3.3 convolution_convert_fusion
  29.3 7.9 %all_to_all.34 = bf16[16,1,129024]{2,1,0:T(2,128)(2,1)} reshape(bf16[576,3584]{1,0:T(8,128)(2,1)} %convolution_convert_fusion) | data formatting | bytes 8257536 | tf_op jit(solution)/shard_map/all_to_all | solution.py:49
  37.2 0.6 broadcast.86
  37.8 26.8 %reduce.9 = bf16[16,129024]{1,0:T(8,128)(2,1)} reduce(bf16[16,1,129024]{2,1,0:T(2,128)(2,1)} %all_to_all.34, bf16[]{:T(256)} %broadcast.86), dimensions={1}, to_apply=%all_to_all.34.reduce_sub_computation | reduce | bytes 8257538 | tf_op jit(solution)/shard_map/all_to_all | solution.py:49
  64.6 6.6 %reshape.140 = bf16[16,2,64512]{2,1,0:T(2,128)(2,1)} reshape(bf16[16,129024]{1,0:T(8,128)(2,1)} %reduce.9) | data formatting | bytes 8257536
  71.2 0.0 all-to-all-done
  71.2 6.7 %all-to-all-start.2 = ((bf16[16,2,64512]{2,1,0:T(2,128)(2,1)}), bf16[16,2,64512]{2,1,0:T(2,128)(2,1)}, u32[]{:S(2)}, u32[]{:S(2)}) async-start(bf16[16,2,64512]{2,1,0:T(2,128)(2,1)} %reshape.140), calls=%async_computation.2 | async-start | bytes 8257536 | tf_op jit(solution)/shard_map/all_to_all | solution.py:49
  77.9 3.2 convolution_convert_fusion.1
  81.1 7.9 %all_to_all.33 = bf16[16,1,129024]{2,1,0:T(2,128)(2,1)} reshape(bf16[576,3584]{1,0:T(8,128)(2,1)} %convolution_convert_fusion.1) | data formatting | bytes 8257536 | tf_op jit(solution)/shard_map/all_to_all | solution.py:50
  89.0 26.7 %reduce.10 = bf16[16,129024]{1,0:T(8,128)(2,1)} reduce(bf16[16,1,129024]{2,1,0:T(2,128)(2,1)} %all_to_all.33, bf16[]{:T(256)} %broadcast.86), dimensions={1}, to_apply=%all_to_all.33.reduce_sub_computation | reduce | bytes 8257538 | tf_op jit(solution)/shard_map/all_to_all | solution.py:50
  115.7 6.6 %reshape.142 = bf16[16,2,64512]{2,1,0:T(2,128)(2,1)} reshape(bf16[16,129024]{1,0:T(8,128)(2,1)} %reduce.10) | data formatting | bytes 8257536
  122.3 31.9 %all-to-all-done.2 = bf16[16,2,64512]{2,1,0:T(2,128)(2,1)} async-done(((bf16[16,2,64512]{2,1,0:T(2,128)(2,1)}), bf16[16,2,64512]{2,1,0:T(2,128)(2,1)}, u32[]{:S(2)}, u32[]{:S(2)}) %all-to-all-start.2) | async-done | bytes 4128800 | tf_op jit(solution)/shard_map/all_to_all | solution.py:49
  154.2 19.6 %all-to-all-start.1 = ((bf16[16,2,64512]{2,1,0:T(2,128)(2,1)}), bf16[16,2,64512]{2,1,0:T(2,128)(2,1)}, u32[]{:S(2)}, u32[]{:S(2)}) async-start(bf16[16,2,64512]{2,1,0:T(2,128)(2,1)} %reshape.142), calls=%async_computation.1 | async-start | bytes 8257536 | tf_op jit(solution)/shard_map/all_to_all | solution.py:50
  173.9 0.1 reshape.107
  174.0 12.2 %reshape.141 = bf16[16,1,129024]{2,1,0:T(2,128)(2,1)} reshape(bf16[16,2,64512]{2,1,0:T(2,128)(2,1)} %all-to-all-done.2) | data formatting | bytes 8257536
  186.1 26.1 %reduce.3 = bf16[16,129024]{1,0:T(8,128)(2,1)} reduce(bf16[16,1,129024]{2,1,0:T(2,128)(2,1)} %reshape.141, bf16[]{:T(256)} %constant.41), dimensions={1}, to_apply=%all_to_all.29.reduce_sub_computation | reduce | bytes 8257538 | tf_op jit(solution)/shard_map/all_to_all | solution.py:49
  212.2 9.0 %reshape.103 = bf16[576,3584]{1,0:T(8,128)(2,1)} reshape(bf16[16,129024]{1,0:T(8,128)(2,1)} %reduce.3) | data formatting | bytes 8257536 | tf_op jit(solution)/shard_map/reshape | solution.py:53
  221.3 5.7 %fusion.2 = f32[576,512]{1,0:T(8,128)S(1)} fusion(bf16[576,3584]{1,0:T(8,128)(2,1)} %reshape.103, bf16[1,3584,512]{2,1,0:T(8,128)(2,1)} %param.12), kind=kOutput, calls=%fused_computation.10 | convolution fusion | flops 2113929216 | bytes 8978432 | tf_op jit(solution)/shard_map/dot_general | solution.py:62
  227.0 3.3 fusion.5
  230.3 19.9 %all-to-all-done.1 = bf16[16,2,64512]{2,1,0:T(2,128)(2,1)} async-done(((bf16[16,2,64512]{2,1,0:T(2,128)(2,1)}), bf16[16,2,64512]{2,1,0:T(2,128)(2,1)}, u32[]{:S(2)}, u32[]{:S(2)}) %all-to-all-start.1) | async-done | bytes 4128800 | tf_op jit(solution)/shard_map/all_to_all | solution.py:50
  250.2 12.2 %reshape.143 = bf16[16,1,129024]{2,1,0:T(2,128)(2,1)} reshape(bf16[16,2,64512]{2,1,0:T(2,128)(2,1)} %all-to-all-done.1) | data formatting | bytes 8257536
  262.4 26.1 %reduce.2 = bf16[16,129024]{1,0:T(8,128)(2,1)} reduce(bf16[16,1,129024]{2,1,0:T(2,128)(2,1)} %reshape.143, bf16[]{:T(256)} %constant.41), dimensions={1}, to_apply=%all_to_all.27.reduce_sub_computation | reduce | bytes 8257538 | tf_op jit(solution)/shard_map/all_to_all | solution.py:50
  288.5 9.3 %reshape.102 = bf16[576,3584]{1,0:T(8,128)(2,1)} reshape(bf16[16,129024]{1,0:T(8,128)(2,1)} %reduce.2) | data formatting | bytes 8257536 | tf_op jit(solution)/shard_map/reshape | solution.py:54
  297.7 6.4 %multiply_convert_fusion.1 = (bf16[576,512]{1,0:T(8,128)(2,1)S(1)}, bf16[576,512]{1,0:T(8,128)(2,1)S(1)}) fusion(f32[576,512]{1,0:T(8,128)S(1)} %fusion.2, f32[576,512]{1,0:T(8,128)} %fusion.5, bf16[576,3584]{1,0:T(8,128)(2,1)} %reshape.102, bf16[1,512,3584]{2,1,0:T(8,128)(2,1)} %param.14, f32[576]{0:T(1024)S(1)} %reshape.107), kind=kOutput, calls=%fused_computation.20 | convolution fusion | flops 2118057984 | bytes 11340032 | tf_op jit(solution)/shard_map/dot_general | solution.py:64
  304.1 0.0 copy-start.7
  304.1 2.4 fusion
  306.5 4.4 add_convert_fusion
  310.9 7.9 %all_to_all.35 = bf16[16,1,129024]{2,1,0:T(2,128)(2,1)} reshape(bf16[576,3584]{1,0:T(8,128)(2,1)} %add_convert_fusion) | data formatting | bytes 8257536 | tf_op jit(solution)/shard_map/all_to_all | solution.py:94
  318.8 26.8 %reduce.11 = bf16[16,129024]{1,0:T(8,128)(2,1)} reduce(bf16[16,1,129024]{2,1,0:T(2,128)(2,1)} %all_to_all.35, bf16[]{:T(256)} %broadcast.86), dimensions={1}, to_apply=%all_to_all.35.reduce_sub_computation | reduce | bytes 8257538 | tf_op jit(solution)/shard_map/all_to_all | solution.py:94
  345.6 6.8 %reshape.144 = bf16[16,2,64512]{2,1,0:T(2,128)(2,1)} reshape(bf16[16,129024]{1,0:T(8,128)(2,1)} %reduce.11) | data formatting | bytes 8257536
  352.4 19.5 %all-to-all-start.3 = ((bf16[16,2,64512]{2,1,0:T(2,128)(2,1)}), bf16[16,2,64512]{2,1,0:T(2,128)(2,1)}, u32[]{:S(2)}, u32[]{:S(2)}) async-start(bf16[16,2,64512]{2,1,0:T(2,128)(2,1)} %reshape.144), calls=%async_computation.3 | async-start | bytes 8257536 | tf_op jit(solution)/shard_map/all_to_all | solution.py:94
  371.9 0.0 reduce-scatter.5.cloned.1.call-start
  372.0 0.3 convolution_convert_fusion.5
  372.3 0.3 convolution_convert_fusion.6
  372.6 3.8 convolution_convert_fusion.2
  376.4 4.3 convolution_convert_fusion.3
  380.7 1.7 pad_maximum_fusion
  382.4 0.0 reduce-scatter.5.cloned.1.call-update
  382.4 0.0 reduce-scatter.3.cloned.1.call-start
  382.5 65.8 %all-to-all-done.3 = bf16[16,2,64512]{2,1,0:T(2,128)(2,1)} async-done(((bf16[16,2,64512]{2,1,0:T(2,128)(2,1)}), bf16[16,2,64512]{2,1,0:T(2,128)(2,1)}, u32[]{:S(2)}, u32[]{:S(2)}) %all-to-all-start.3) | async-done | bytes 4128800 | tf_op jit(solution)/shard_map/all_to_all | solution.py:94
  448.3 12.2 %reshape.145 = bf16[16,1,129024]{2,1,0:T(2,128)(2,1)} reshape(bf16[16,2,64512]{2,1,0:T(2,128)(2,1)} %all-to-all-done.3) | data formatting | bytes 8257536
  460.5 26.1 %reduce.4 = bf16[16,129024]{1,0:T(8,128)(2,1)} reduce(bf16[16,1,129024]{2,1,0:T(2,128)(2,1)} %reshape.145, bf16[]{:T(256)} %constant.41), dimensions={1}, to_apply=%all_to_all.31.reduce_sub_computation | reduce | bytes 8257538 | tf_op jit(solution)/shard_map/all_to_all | solution.py:94
  486.6 9.1 %reshape.104 = bf16[576,3584]{1,0:T(8,128)(2,1)} reshape(bf16[16,129024]{1,0:T(8,128)(2,1)} %reduce.4) | data formatting | bytes 8257536 | tf_op jit(solution)/shard_map/reshape | solution.py:102
  495.7 3.8 convolution_convert_fusion.4
  499.5 0.0 reduce-scatter.3.cloned.1.call-update
  499.5 0.0 reduce-scatter.5.cloned.1.call-done
  499.6 2.9 copy.36
  502.5 25.9 %reduce-scatter.3.cloned.1.call-done = bf16[64,1792]{1,0:T(8,128)(2,1)} async-done(((bf16[64,3584]{1,0:T(8,128)(2,1)}), bf16[64,1792]{1,0:T(8,128)(2,1)}) %reduce-scatter.3.cloned.1.call-update) | async-done | bytes 229392 | tf_op jit(solution)/shard_map/reduce_scatter | solution.py:104
  (25 shorter events, 0.1 us)
Async XLA Ops:
  7.2 18.9 %copy-start = (bf16[64,3584]{1,0:T(8,128)(2,1)S(1)}, bf16[64,3584]{1,0:T(8,128)(2,1)}, u32[]{:S(2)}) copy-start(bf16[64,3584]{1,0:T(8,128)(2,1)} %param.8) | copy-start | bytes 1376260
  18.6 52.6 %all-to-all-start = ((bf16[16,1,36]{2,1,0:T(2,128)(2,1)}), bf16[16,1,36]{2,1,0:T(2,128)(2,1)S(1)}, u32[]{:S(2)}, u32[]{:S(2)}) async-start(bf16[16,1,36]{2,1,0:T(2,128)(2,1)} %all_to_all.32), calls=%async_computation | async-start | bytes 16384 | tf_op jit(solution)/shard_map/all_to_all | solution.py:51
  71.2 6.7 %copy-start.4 = (bf16[64,3584]{1,0:T(8,128)(2,1)S(1)}, bf16[64,3584]{1,0:T(8,128)(2,1)}, u32[]{:S(2)}) copy-start(bf16[64,3584]{1,0:T(8,128)(2,1)} %param.9) | copy-start | bytes 1376260
  71.2 83.1 %all-to-all-start.2 = ((bf16[16,2,64512]{2,1,0:T(2,128)(2,1)}), bf16[16,2,64512]{2,1,0:T(2,128)(2,1)}, u32[]{:S(2)}, u32[]{:S(2)}) async-start(bf16[16,2,64512]{2,1,0:T(2,128)(2,1)} %reshape.140), calls=%async_computation.2 | async-start | bytes 8257536 | tf_op jit(solution)/shard_map/all_to_all | solution.py:49
  154.2 96.0 %all-to-all-start.1 = ((bf16[16,2,64512]{2,1,0:T(2,128)(2,1)}), bf16[16,2,64512]{2,1,0:T(2,128)(2,1)}, u32[]{:S(2)}, u32[]{:S(2)}) async-start(bf16[16,2,64512]{2,1,0:T(2,128)(2,1)} %reshape.142), calls=%async_computation.1 | async-start | bytes 8257536 | tf_op jit(solution)/shard_map/all_to_all | solution.py:50
  221.3 5.7 %copy-start.2 = (bf16[576,3584]{1,0:T(8,128)(2,1)S(1)}, bf16[576,3584]{1,0:T(8,128)(2,1)}, u32[]{:S(2)}) copy-start(bf16[576,3584]{1,0:T(8,128)(2,1)} %reshape.103) | copy-start | bytes 12386308
  221.3 5.7 %copy-start.6 = (bf16[1,3584,512]{2,1,0:T(8,128)(2,1)S(1)}, bf16[1,3584,512]{2,1,0:T(8,128)(2,1)}, u32[]{:S(2)}) copy-start(bf16[1,3584,512]{2,1,0:T(8,128)(2,1)} %param.13) | copy-start | bytes 11010052
  227.0 70.7 %copy-start.8 = (f32[576,512]{1,0:T(8,128)}, f32[576,512]{1,0:T(8,128)S(1)}, u32[]{:S(2)}) copy-start(f32[576,512]{1,0:T(8,128)S(1)} %fusion.2) | copy-start | bytes 3538948
  297.7 6.4 %copy-start.5 = (bf16[1,3584,512]{2,1,0:T(8,128)(2,1)S(1)}, bf16[1,3584,512]{2,1,0:T(8,128)(2,1)}, u32[]{:S(2)}) copy-start(bf16[1,3584,512]{2,1,0:T(8,128)(2,1)} %param.12) | copy-start | bytes 11010052
  304.1 2.4 copy-start.7
  352.4 19.6 %copy-start.3 = (bf16[1,512,128]{2,1,0:T(8,128)(2,1)S(1)}, bf16[1,512,128]{2,1,0:T(8,128)(2,1)}, u32[]{:S(2)}) copy-start(bf16[1,512,128]{2,1,0:T(8,128)(2,1)} %param.15) | copy-start | bytes 393220
  352.4 96.0 %all-to-all-start.3 = ((bf16[16,2,64512]{2,1,0:T(2,128)(2,1)}), bf16[16,2,64512]{2,1,0:T(2,128)(2,1)}, u32[]{:S(2)}, u32[]{:S(2)}) async-start(bf16[16,2,64512]{2,1,0:T(2,128)(2,1)} %reshape.144), calls=%async_computation.3 | async-start | bytes 8257536 | tf_op jit(solution)/shard_map/all_to_all | solution.py:94
  371.9 127.6 %reduce-scatter.5.cloned.1.call-start = ((), (), s32[]{:S(2)}) async-start(), calls=%async_computation.7 | async-start | bytes 4128768 | tf_op jit(solution)/shard_map/reduce_scatter | solution.py:87
  382.4 145.9 %reduce-scatter.3.cloned.1.call-start = ((), (), s32[]{:S(2)}) async-start(), calls=%async_computation.6 | async-start | bytes 688128 | tf_op jit(solution)/shard_map/reduce_scatter | solution.py:104
  486.6 41.7 %copy-start.1 = (bf16[64,3584]{1,0:T(8,128)(2,1)S(1)}, bf16[64,3584]{1,0:T(8,128)(2,1)}, u32[]{:S(2)}) copy-start(bf16[64,3584]{1,0:T(8,128)(2,1)} %param.8) | copy-start | bytes 1376260
Sparse Core Ops, SparseCore 0:
  382.6 40.3 reduce-scatter.4
  499.7 28.6 reduce-scatter.2
where the time goes:
time: 544 us; the launch traced here: 536 us
  other arithmetic  162 us (30%)
  waiting for transfers between devices  144 us (26%)
  local copies, waits for them, and re-layouts  121 us (22%)
  starting transfers between devices  53.3 us (10%)
  matrix products  41.2 us (8%)
  between operations  14.7 us (3%)
    all_to_all x1, waiting for transfers between devices, on_device(): lax.all_to_all(part_rows.reshape(expert_count, capacity * model_width), '...  65.8 us
    unnamed x27, local copies, waits for them, and re-layouts  61 us
    all_to_all x2, other arithmetic, on_device(): lax.all_to_all(part_rows.reshape(expert_count, capacity * model_width), '...  52.9 us
    all_to_all x2, other arithmetic, on_device(): lax.all_to_all(to_slots(saved_inputs), 'expert', split_axis=0, concat_axi...  52.8 us
    all_to_all x2, other arithmetic, on_device(): lax.all_to_all(to_slots(output_grad), 'expert', split_axis=0, concat_axis...  52.8 us
    all_to_all x1, waiting for transfers between devices, on_device(): lax.all_to_all(to_slots(saved_inputs), 'expert', split_axis=0, concat_axi...  31.9 us
    reduce_scatter x1, waiting for transfers between devices, on_device(): lax.psum_scatter(spread.astype(jnp.bfloat16), 'dp', scatter_dimension=1,...  25.9 us
    all_to_all x1, waiting for transfers between devices, on_device(): lax.all_to_all(to_slots(output_grad), 'expert', split_axis=0, concat_axis...  19.9 us
  transfers between devices with their start and end apart: 6, of which 4 were waited for; matrix products, arithmetic and copies ran while one was open for 36% of the time, Pallas kernels for 0%

commit v1 on v0

--- a/solution.py
+++ b/solution.py
@@ -2,6 +2,22 @@
 import jax.numpy as jnp
 from jax import lax
 from jax.sharding import PartitionSpec as P
+
+
+def pairwise_exchange(value, axis, split, join):
+    ways, here = (lax.axis_size(axis), lax.axis_index(axis))
+    width = value.shape[split] // ways
+    lengths = list(value.shape)
+    lengths[split] = width
+    height = lengths[join]
+    lengths[join] = height * ways
+    full = jnp.zeros(lengths, value.dtype)
+    for mask in range(ways):
+        part = lax.dynamic_slice_in_dim(value, (here ^ mask) * width, width, axis=split)
+        if mask:
+            part = lax.ppermute(part, axis, [(d, d ^ mask) for d in range(ways)])
+        full = lax.dynamic_update_slice_in_dim(full, part, (here ^ mask) * height, axis=join)
+    return full
 
 
 def on_device(
@@ -46,7 +62,7 @@
         return picked.reshape(expert_count, capacity * source_rows.shape[1])
 
     recv_inputs, recv_grads, recv_gates = (
-        lax.all_to_all(to_slots(saved_inputs), "expert", split_axis=0, concat_axis=0, tiled=True),
+        pairwise_exchange(to_slots(saved_inputs), "expert", 0, 0),
         lax.all_to_all(to_slots(output_grad), "expert", split_axis=0, concat_axis=0, tiled=True),
         lax.all_to_all(gate_slots, "expert", split_axis=0, concat_axis=0, tiled=True),
     )

time: 544 us -> 762 us (1.40)
  local copies, waits for them, and re-layouts: 121 us -> 294 us
  waiting for transfers between devices: 144 us -> 234 us
  other arithmetic: 162 us -> 109 us
  starting transfers between devices: 53.3 us -> 61.4 us
    dynamic_update_slice x0 -> x16, local copies, waits for them, and re-layouts: none -> 165 us  [pairwise_exchange(): lax.dynamic_update_slice_in_dim(full, part, (here ^ mask) * height, axis=...]
    ppermute x0 -> x15, waiting for transfers between devices: none -> 142 us  [pairwise_exchange(): part = lax.ppermute(part, axis, [(d, d ^ mask) for d in range(ways)])]
    all_to_all x2 -> x0, other arithmetic: 52.8 us -> none  [on_device(): lax.all_to_all(to_slots(saved_inputs), 'expert', split_axis=0, concat_axi...]
    ppermute x0 -> x15, starting transfers between devices: none -> 41.6 us  [pairwise_exchange(): part = lax.ppermute(part, axis, [(d, d ^ mask) for d in range(ways)])]
    all_to_all x1 -> x0, waiting for transfers between devices: 31.9 us -> none  [on_device(): lax.all_to_all(to_slots(saved_inputs), 'expert', split_axis=0, concat_axi...]
    dynamic_slice x0 -> x1, local copies, waits for them, and re-layouts: none -> 22.1 us  [pairwise_exchange(): lax.dynamic_slice_in_dim(value, (here ^ mask) * width, width, axis=split)]
    all_to_all x1, waiting for transfers between devices: 19.9 us -> 0.01 us  [on_device(): lax.all_to_all(to_slots(output_grad), 'expert', split_axis=0, concat_axis...]
    unnamed x27 -> x61, local copies, waits for them, and re-layouts: 61 us -> 42.8 us
  transfers between devices with their start and end apart: 6 -> 20, of which waited for: 4 -> 9; matrix products, arithmetic and copies ran while one was open for 36% -> 43% of each run, Pallas kernels for 0% -> 0%
where the time goes in v1:
time: 762 us; the launch traced here: 754 us
  local copies, waits for them, and re-layouts  294 us (39%)
  waiting for transfers between devices  234 us (31%)
  other arithmetic  109 us (14%)
  starting transfers between devices  61.4 us (8%)
  matrix products  41.1 us (5%)
  between operations  14.6 us (2%)
    dynamic_update_slice x16, local copies, waits for them, and re-layouts, pairwise_exchange(): lax.dynamic_update_slice_in_dim(full, part, (here ^ mask) * height, axis=...  165 us
    ppermute x15, waiting for transfers between devices, pairwise_exchange(): part = lax.ppermute(part, axis, [(d, d ^ mask) for d in range(ways)])  142 us
    all_to_all x1, waiting for transfers between devices, on_device(): lax.all_to_all(part_rows.reshape(expert_count, capacity * model_width), '...  65.7 us
    all_to_all x2, other arithmetic, on_device(): lax.all_to_all(to_slots(output_grad), 'expert', split_axis=0, concat_axis...  52.8 us
    all_to_all x2, other arithmetic, on_device(): lax.all_to_all(part_rows.reshape(expert_count, capacity * model_width), '...  52.8 us
    unnamed x61, local copies, waits for them, and re-layouts  42.8 us
    ppermute x15, starting transfers between devices, pairwise_exchange(): part = lax.ppermute(part, axis, [(d, d ^ mask) for d in range(ways)])  41.6 us
    reduce_scatter x1, waiting for transfers between devices, on_device(): lax.psum_scatter(spread.astype(jnp.bfloat16), 'dp', scatter_dimension=1,...  25.9 us
  transfers between devices with their start and end apart: 20, of which 9 were waited for; matrix products, arithmetic and copies ran while one was open for 43% of the time, Pallas kernels for 0%

profile of v1, /device:TPU:0, one launch (start us, length us, event | category | flops | bytes accessed | tf_op | source)
XLA Modules:
  0.0 753.8 jit_solution(6068990573552911849)
XLA Ops:
  10.6 2.4 scatter_custom_fusion
  14.0 3.9 gather_fusion
  18.7 7.9 %all-to-all-start = ((bf16[16,1,36]{2,1,0:T(2,128)(2,1)}), bf16[16,1,36]{2,1,0:T(2,128)(2,1)S(1)}, u32[]{:S(2)}, u32[]{:S(2)}) async-start(bf16[16,1,36]{2,1,0:T(2,128)(2,1)} %all_to_all.24), calls=%async_computation | async-start | bytes 16384 | tf_op jit(solution)/shard_map/all_to_all | solution.py:67
  26.7 3.2 convolution_convert_fusion
  29.9 3.2 convolution_convert_fusion.1
  33.1 9.1 %reshape.101 = bf16[16,129024]{1,0:T(8,128)(2,1)} reshape(bf16[576,3584]{1,0:T(8,128)(2,1)} %convolution_convert_fusion) | data formatting | bytes 8257536 | tf_op jit(solution)/shard_map/reshape | solution.py:62
  42.2 8.0 %all_to_all.25 = bf16[16,1,129024]{2,1,0:T(2,128)(2,1)} reshape(bf16[576,3584]{1,0:T(8,128)(2,1)} %convolution_convert_fusion.1) | data formatting | bytes 8257536 | tf_op jit(solution)/shard_map/all_to_all | solution.py:66
  50.7 26.7 %reduce.8 = bf16[16,129024]{1,0:T(8,128)(2,1)} reduce(bf16[16,1,129024]{2,1,0:T(2,128)(2,1)} %all_to_all.25, bf16[]{:T(256)} %broadcast.89), dimensions={1}, to_apply=%all_to_all.25.reduce_sub_computation | reduce | bytes 8257538 | tf_op jit(solution)/shard_map/all_to_all | solution.py:66
  77.4 6.6 reshape.138
  84.6 6.3 all-to-all-start.1
  90.9 22.1 %constant_dynamic-slice_fusion = (bf16[1,129024]{1,0:T(2,128)(2,1)S(1)}, bf16[1,129024]{1,0:T(2,128)(2,1)S(1)}, bf16[1,129024]{1,0:T(2,128)(2,1)S(1)}, bf16[1,12...) fusion(bf16[16,129024]{1,0:T(8,128)(2,1)} %reshape.101, ...), kind=kLoop, calls=%fused_computation.62 | loop fusion | bytes 8257600 | tf_op jit(solution)/shard_map/dynamic_slice | solution.py:16
  115.2 1.7 collective-permute-start.3
  117.1 2.5 collective-permute-start.5
  119.6 16.6 %collective-permute-done.1 = bf16[1,129024]{1,0:T(2,128)(2,1)S(1)} collective-permute-done((bf16[1,129024]{1,0:T(2,128)(2,1)S(1)}, bf16[1,129024]{1,0:T(2,128)(2,1)S(1)}, u32[]{:S(2)}, u32[]{:S(2)}) %collective-permute-start.1) | collective-permute-done | bytes 258080 | tf_op jit(solution)/shard_map/ppermute | solution.py:18
  136.3 18.6 %collective-permute-done.2 = bf16[1,129024]{1,0:T(2,128)(2,1)S(1)} collective-permute-done((bf16[1,129024]{1,0:T(2,128)(2,1)S(1)}, bf16[1,129024]{1,0:T(2,128)(2,1)S(1)}, u32[]{:S(2)}, u32[]{:S(2)}) %collective-permute-start.2) | collective-permute-done | bytes 258080 | tf_op jit(solution)/shard_map/ppermute | solution.py:18
  154.9 14.9 %collective-permute-done.3 = bf16[1,129024]{1,0:T(2,128)(2,1)S(1)} collective-permute-done((bf16[1,129024]{1,0:T(2,128)(2,1)S(1)}, bf16[1,129024]{1,0:T(2,128)(2,1)S(1)}, u32[]{:S(2)}, u32[]{:S(2)}) %collective-permute-start.3) | collective-permute-done | bytes 258080 | tf_op jit(solution)/shard_map/ppermute | solution.py:18
  169.8 3.3 collective-permute-start.8
  173.1 8.8 %collective-permute-done.4 = bf16[1,129024]{1,0:T(2,128)(2,1)S(1)} collective-permute-done((bf16[1,129024]{1,0:T(2,128)(2,1)S(1)}, bf16[1,129024]{1,0:T(2,128)(2,1)S(1)}, u32[]{:S(2)}, u32[]{:S(2)}) %collective-permute-start.4) | collective-permute-done | bytes 258080 | tf_op jit(solution)/shard_map/ppermute | solution.py:18
  181.9 25.0 %collective-permute-start.9 = (bf16[1,129024]{1,0:T(2,128)(2,1)S(1)}, bf16[1,129024]{1,0:T(2,128)(2,1)S(1)}, u32[]{:S(2)}, u32[]{:S(2)}) collective-permute-start(bf16[1,129024]{1,0:T(2,128)(2,1)S(1)} %get-tuple-element.17), channel_id=1, source_target_pairs={{0,10},{1,11},{2,8},{3,9},{4,14},{5,15},{6,12},{7,13},{8,2},{9,3},... | collective-permute-start | bytes 774152 | tf_op jit(solution)/shard_map/ppermute | solution.py:18
  207.0 11.4 %collective-permute-done.5 = bf16[1,129024]{1,0:T(2,128)(2,1)S(1)} collective-permute-done((bf16[1,129024]{1,0:T(2,128)(2,1)S(1)}, bf16[1,129024]{1,0:T(2,128)(2,1)S(1)}, u32[]{:S(2)}, u32[]{:S(2)}) %collective-permute-start.5) | collective-permute-done | bytes 258080 | tf_op jit(solution)/shard_map/ppermute | solution.py:18
  218.4 9.9 %collective-permute-done.6 = bf16[1,129024]{1,0:T(2,128)(2,1)S(1)} collective-permute-done((bf16[1,129024]{1,0:T(2,128)(2,1)S(1)}, bf16[1,129024]{1,0:T(2,128)(2,1)S(1)}, u32[]{:S(2)}, u32[]{:S(2)}) %collective-permute-start.6) | collective-permute-done | bytes 258080 | tf_op jit(solution)/shard_map/ppermute | solution.py:18
  228.3 2.3 collective-permute-start.11
  231.8 2.5 collective-permute-start.13
  234.3 61.9 %collective-permute-done.9 = bf16[1,129024]{1,0:T(2,128)(2,1)S(1)} collective-permute-done((bf16[1,129024]{1,0:T(2,128)(2,1)S(1)}, bf16[1,129024]{1,0:T(2,128)(2,1)S(1)}, u32[]{:S(2)}, u32[]{:S(2)}) %collective-permute-start.9) | collective-permute-done | bytes 258080 | tf_op jit(solution)/shard_map/ppermute | solution.py:18
  297.0 2.2 broadcast_in_dim.17
  299.2 10.3 %dynamic_update_slice.48 = bf16[16,129024]{1,0:T(8,128)(2,1)} dynamic-update-slice(bf16[16,129024]{1,0:T(8,128)(2,1)} %broadcast_in_dim.17, bf16[1,129024]{1,0:T(2,128)(2,1)S(1)} %get-tuple-element.27, s32[]{:T(128)S(6)} %select_n.90, s32[]{:T(128)} %constant.27.clone.1) | dynamic-update-slice | bytes 516100 | tf_op jit(solution)/shard_map/dynamic_update_slice | solution.py:19
  309.6 10.4 %dynamic_update_slice.49 = bf16[16,129024]{1,0:T(8,128)(2,1)} dynamic-update-slice(bf16[16,129024]{1,0:T(8,128)(2,1)} %dynamic_update_slice.48, bf16[1,129024]{1,0:T(2,128)(2,1)} %copy-done.4, s32[]{:T(128)S(6)} %select_n.91, s32[]{:T(128)} %constant.27.clone.1) | dynamic-update-slice | bytes 516100 | tf_op jit(solution)/shard_map/dynamic_update_slice | solution.py:19
  320.0 10.3 %dynamic_update_slice.50 = bf16[16,129024]{1,0:T(8,128)(2,1)} dynamic-update-slice(bf16[16,129024]{1,0:T(8,128)(2,1)} %dynamic_update_slice.49, bf16[1,129024]{1,0:T(2,128)(2,1)} %copy-done.5, s32[]{:T(128)S(6)} %select_n.92, s32[]{:T(128)} %constant.27.clone.1) | dynamic-update-slice | bytes 516100 | tf_op jit(solution)/shard_map/dynamic_update_slice | solution.py:19
  330.4 10.3 %dynamic_update_slice.51 = bf16[16,129024]{1,0:T(8,128)(2,1)} dynamic-update-slice(bf16[16,129024]{1,0:T(8,128)(2,1)} %dynamic_update_slice.50, bf16[1,129024]{1,0:T(2,128)(2,1)} %copy-done.6, s32[]{:T(128)S(6)} %select_n.93, s32[]{:T(128)} %constant.27.clone.1) | dynamic-update-slice | bytes 516100 | tf_op jit(solution)/shard_map/dynamic_update_slice | solution.py:19
  340.7 10.3 %dynamic_update_slice.52 = bf16[16,129024]{1,0:T(8,128)(2,1)} dynamic-update-slice(bf16[16,129024]{1,0:T(8,128)(2,1)} %dynamic_update_slice.51, bf16[1,129024]{1,0:T(2,128)(2,1)} %copy-done.7, s32[]{:T(128)S(6)} %select_n.94, s32[]{:T(128)} %constant.27.clone.1) | dynamic-update-slice | bytes 516100 | tf_op jit(solution)/shard_map/dynamic_update_slice | solution.py:19
  351.0 10.3 %dynamic_update_slice.53 = bf16[16,129024]{1,0:T(8,128)(2,1)} dynamic-update-slice(bf16[16,129024]{1,0:T(8,128)(2,1)} %dynamic_update_slice.52, bf16[1,129024]{1,0:T(2,128)(2,1)S(1)} %copy-done.9, s32[]{:T(128)S(6)} %select_n.95, s32[]{:T(128)} %constant.27.clone.1) | dynamic-update-slice | bytes 516100 | tf_op jit(solution)/shard_map/dynamic_update_slice | solution.py:19
  361.3 10.4 %dynamic_update_slice.54 = bf16[16,129024]{1,0:T(8,128)(2,1)} dynamic-update-slice(bf16[16,129024]{1,0:T(8,128)(2,1)} %dynamic_update_slice.53, bf16[1,129024]{1,0:T(2,128)(2,1)} %copy-done.10, s32[]{:T(128)S(6)} %select_n.96, s32[]{:T(128)} %constant.27.clone.1) | dynamic-update-slice | bytes 516100 | tf_op jit(solution)/shard_map/dynamic_update_slice | solution.py:19
  371.7 10.3 %dynamic_update_slice.55 = bf16[16,129024]{1,0:T(8,128)(2,1)} dynamic-update-slice(bf16[16,129024]{1,0:T(8,128)(2,1)} %dynamic_update_slice.54, bf16[1,129024]{1,0:T(2,128)(2,1)} %copy-done.11, s32[]{:T(128)S(6)} %select_n.97, s32[]{:T(128)} %constant.27.clone.1) | dynamic-update-slice | bytes 516100 | tf_op jit(solution)/shard_map/dynamic_update_slice | solution.py:19
  382.1 10.3 %dynamic_update_slice.56 = bf16[16,129024]{1,0:T(8,128)(2,1)} dynamic-update-slice(bf16[16,129024]{1,0:T(8,128)(2,1)} %dynamic_update_slice.55, bf16[1,129024]{1,0:T(2,128)(2,1)} %copy-done.12, s32[]{:T(128)S(6)} %select_n.98, s32[]{:T(128)} %constant.27.clone.1) | dynamic-update-slice | bytes 516100 | tf_op jit(solution)/shard_map/dynamic_update_slice | solution.py:19
  392.4 10.3 %dynamic_update_slice.57 = bf16[16,129024]{1,0:T(8,128)(2,1)} dynamic-update-slice(bf16[16,129024]{1,0:T(8,128)(2,1)} %dynamic_update_slice.56, bf16[1,129024]{1,0:T(2,128)(2,1)} %copy-done.13, s32[]{:T(128)S(6)} %select_n.99, s32[]{:T(128)} %constant.27.clone.1) | dynamic-update-slice | bytes 516100 | tf_op jit(solution)/shard_map/dynamic_update_slice | solution.py:19
  402.7 10.3 %dynamic_update_slice.58 = bf16[16,129024]{1,0:T(8,128)(2,1)} dynamic-update-slice(bf16[16,129024]{1,0:T(8,128)(2,1)} %dynamic_update_slice.57, bf16[1,129024]{1,0:T(2,128)(2,1)S(1)} %copy-done.15, s32[]{:T(128)S(6)} %select_n.100, s32[]{:T(128)} %constant.27.clone.1) | dynamic-update-slice | bytes 516100 | tf_op jit(solution)/shard_map/dynamic_update_slice | solution.py:19
  413.0 10.3 %dynamic_update_slice.59 = bf16[16,129024]{1,0:T(8,128)(2,1)} dynamic-update-slice(bf16[16,129024]{1,0:T(8,128)(2,1)} %dynamic_update_slice.58, bf16[1,129024]{1,0:T(2,128)(2,1)} %collective-permute-done.10, s32[]{:T(128)S(6)} %select_n.101, s32[]{:T(128)} %constant.27.clone.1) | dynamic-update-slice | bytes 516100 | tf_op jit(solution)/shard_map/dynamic_update_slice | solution.py:19
  423.3 10.3 %dynamic_update_slice.60 = bf16[16,129024]{1,0:T(8,128)(2,1)} dynamic-update-slice(bf16[16,129024]{1,0:T(8,128)(2,1)} %dynamic_update_slice.59, bf16[1,129024]{1,0:T(2,128)(2,1)} %collective-permute-done.11, s32[]{:T(128)S(6)} %select_n.102, s32[]{:T(128)} %constant.27.clone.1) | dynamic-update-slice | bytes 516100 | tf_op jit(solution)/shard_map/dynamic_update_slice | solution.py:19
  433.6 10.3 %dynamic_update_slice.61 = bf16[16,129024]{1,0:T(8,128)(2,1)} dynamic-update-slice(bf16[16,129024]{1,0:T(8,128)(2,1)} %dynamic_update_slice.60, bf16[1,129024]{1,0:T(2,128)(2,1)} %collective-permute-done.12, s32[]{:T(128)S(6)} %select_n.103, s32[]{:T(128)} %constant.27.clone.1) | dynamic-update-slice | bytes 516100 | tf_op jit(solution)/shard_map/dynamic_update_slice | solution.py:19
  444.0 10.3 %dynamic_update_slice.62 = bf16[16,129024]{1,0:T(8,128)(2,1)} dynamic-update-slice(bf16[16,129024]{1,0:T(8,128)(2,1)} %dynamic_update_slice.61, bf16[1,129024]{1,0:T(2,128)(2,1)} %collective-permute-done.13, s32[]{:T(128)S(6)} %select_n.104, s32[]{:T(128)} %constant.27.clone.1) | dynamic-update-slice | bytes 516100 | tf_op jit(solution)/shard_map/dynamic_update_slice | solution.py:19
  454.3 10.3 %dynamic_update_slice.63 = bf16[16,129024]{1,0:T(8,128)(2,1)} dynamic-update-slice(bf16[16,129024]{1,0:T(8,128)(2,1)} %dynamic_update_slice.62, bf16[1,129024]{1,0:T(2,128)(2,1)} %collective-permute-done.14, s32[]{:T(128)S(6)} %select_n.105, s32[]{:T(128)} %constant.27.clone.1) | dynamic-update-slice | bytes 516100 | tf_op jit(solution)/shard_map/dynamic_update_slice | solution.py:19
  464.6 9.2 %reshape.102 = bf16[576,3584]{1,0:T(8,128)(2,1)} reshape(bf16[16,129024]{1,0:T(8,128)(2,1)} %dynamic_update_slice.63) | data formatting | bytes 8257536 | tf_op jit(solution)/shard_map/reshape | solution.py:69
  473.9 5.7 fusion.2
  479.6 3.3 fusion.5
  482.9 12.2 %reshape.139 = bf16[16,1,129024]{2,1,0:T(2,128)(2,1)} reshape(bf16[16,2,64512]{2,1,0:T(2,128)(2,1)} %all-to-all-done.1) | data formatting | bytes 8257536
  495.1 26.1 %reduce.2 = bf16[16,129024]{1,0:T(8,128)(2,1)} reduce(bf16[16,1,129024]{2,1,0:T(2,128)(2,1)} %reshape.139, bf16[]{:T(256)} %constant.74), dimensions={1}, to_apply=%all_to_all.21.reduce_sub_computation | reduce | bytes 8257538 | tf_op jit(solution)/shard_map/all_to_all | solution.py:66
  521.2 9.4 %reshape.100 = bf16[576,3584]{1,0:T(8,128)(2,1)} reshape(bf16[16,129024]{1,0:T(8,128)(2,1)} %reduce.2) | data formatting | bytes 8257536 | tf_op jit(solution)/shard_map/reshape | solution.py:70
  530.6 6.4 multiply_convert_fusion.1
  537.0 2.4 fusion
  539.4 4.4 add_convert_fusion
  543.8 8.0 %all_to_all.26 = bf16[16,1,129024]{2,1,0:T(2,128)(2,1)} reshape(bf16[576,3584]{1,0:T(8,128)(2,1)} %add_convert_fusion) | data formatting | bytes 8257536 | tf_op jit(solution)/shard_map/all_to_all | solution.py:110
  551.8 26.7 %reduce.9 = bf16[16,129024]{1,0:T(8,128)(2,1)} reduce(bf16[16,1,129024]{2,1,0:T(2,128)(2,1)} %all_to_all.26, bf16[]{:T(256)} %broadcast.89), dimensions={1}, to_apply=%all_to_all.26.reduce_sub_computation | reduce | bytes 8257538 | tf_op jit(solution)/shard_map/all_to_all | solution.py:110
  578.5 6.6 reshape.140
  585.0 5.3 all-to-all-start.2
  591.2 3.8 convolution_convert_fusion.2
  595.0 4.3 convolution_convert_fusion.3
  599.3 1.7 pad_maximum_fusion
  601.1 65.7 %all-to-all-done.2 = bf16[16,2,64512]{2,1,0:T(2,128)(2,1)} async-done(((bf16[16,2,64512]{2,1,0:T(2,128)(2,1)}), bf16[16,2,64512]{2,1,0:T(2,128)(2,1)}, u32[]{:S(2)}, u32[]{:S(2)}) %all-to-all-start.2) | async-done | bytes 4128800 | tf_op jit(solution)/shard_map/all_to_all | solution.py:110
  666.7 12.2 %reshape.141 = bf16[16,1,129024]{2,1,0:T(2,128)(2,1)} reshape(bf16[16,2,64512]{2,1,0:T(2,128)(2,1)} %all-to-all-done.2) | data formatting | bytes 8257536
  678.9 26.1 %reduce.3 = bf16[16,129024]{1,0:T(8,128)(2,1)} reduce(bf16[16,1,129024]{2,1,0:T(2,128)(2,1)} %reshape.141, bf16[]{:T(256)} %constant.74), dimensions={1}, to_apply=%all_to_all.23.reduce_sub_computation | reduce | bytes 8257538 | tf_op jit(solution)/shard_map/all_to_all | solution.py:110
  705.0 9.1 %reshape.103 = bf16[576,3584]{1,0:T(8,128)(2,1)} reshape(bf16[16,129024]{1,0:T(8,128)(2,1)} %reduce.3) | data formatting | bytes 8257536 | tf_op jit(solution)/shard_map/reshape | solution.py:118
  714.1 3.8 convolution_convert_fusion.4
  718.0 2.9 copy.34
  720.9 25.9 %reduce-scatter.3.cloned.1.call-done = bf16[64,1792]{1,0:T(8,128)(2,1)} async-done(((bf16[64,3584]{1,0:T(8,128)(2,1)}), bf16[64,1792]{1,0:T(8,128)(2,1)}) %reduce-scatter.3.cloned.1.call-update) | async-done | bytes 229392 | tf_op jit(solution)/shard_map/reduce_scatter | solution.py:120
  (103 shorter events, 11.7 us)
Async XLA Ops:
  7.2 19.5 %copy-start = (bf16[64,3584]{1,0:T(8,128)(2,1)S(1)}, bf16[64,3584]{1,0:T(8,128)(2,1)}, u32[]{:S(2)}) copy-start(bf16[64,3584]{1,0:T(8,128)(2,1)} %param.8) | copy-start | bytes 1376260
  13.1 16.8 %copy-start.17 = (s32[576]{0:T(1024)}, s32[576]{0:T(1024)S(1)}, u32[]{:S(2)}) copy-start(s32[576]{0:T(1024)S(1)} %get-tuple-element.31) | copy-start | bytes 6916
  17.9 12.0 %copy-start.16 = (bf16[64,3584]{1,0:T(8,128)(2,1)S(1)}, bf16[64,3584]{1,0:T(8,128)(2,1)}, u32[]{:S(2)}) copy-start(bf16[64,3584]{1,0:T(8,128)(2,1)} %param.9) | copy-start | bytes 1376260
  17.9 15.2 %copy-start.19 = (pred[576]{0:T(1024)(128)(4,1)}, pred[576]{0:T(1024)(128)(4,1)S(1)}, u32[]{:S(2)}) copy-start(pred[576]{0:T(1024)(128)(4,1)S(1)} %get-tuple-element.11) | copy-start | bytes 1732
  18.7 65.3 %all-to-all-start = ((bf16[16,1,36]{2,1,0:T(2,128)(2,1)}), bf16[16,1,36]{2,1,0:T(2,128)(2,1)S(1)}, u32[]{:S(2)}, u32[]{:S(2)}) async-start(bf16[16,1,36]{2,1,0:T(2,128)(2,1)} %all_to_all.24), calls=%async_computation | async-start | bytes 16384 | tf_op jit(solution)/shard_map/all_to_all | solution.py:67
  84.0 0.6 copy-start.21
  84.6 398.3 %all-to-all-start.1 = ((bf16[16,2,64512]{2,1,0:T(2,128)(2,1)}), bf16[16,2,64512]{2,1,0:T(2,128)(2,1)}, u32[]{:S(2)}, u32[]{:S(2)}) async-start(bf16[16,2,64512]{2,1,0:T(2,128)(2,1)} %reshape.138), calls=%async_computation.1 | async-start | bytes 8257536 | tf_op jit(solution)/shard_map/all_to_all | solution.py:66
  113.0 196.5 %copy-start.22 = (bf16[16,1,36]{2,1,0:T(2,128)(2,1)S(1)}, bf16[16,1,36]{2,1,0:T(2,128)(2,1)}, u32[]{:S(2)}) copy-start(bf16[16,1,36]{2,1,0:T(2,128)(2,1)} %copy-done.21) | copy-start | bytes 3460
  113.0 4.1 collective-permute-start
  113.6 22.7 %collective-permute-start.1 = (bf16[1,129024]{1,0:T(2,128)(2,1)S(1)}, bf16[1,129024]{1,0:T(2,128)(2,1)S(1)}, u32[]{:S(2)}, u32[]{:S(2)}) collective-permute-start(bf16[1,129024]{1,0:T(2,128)(2,1)S(1)} %get-tuple-element.25), channel_id=1, source_target_pairs={{0,2},{1,3},{2,0},{3,1},{4,6},{5,7},{6,4},{7,5},{8,10},{9,11},{10,... | collective-permute-start | bytes 774152 | tf_op jit(solution)/shard_map/ppermute | solution.py:18
  115.2 39.7 %collective-permute-start.2 = (bf16[1,129024]{1,0:T(2,128)(2,1)S(1)}, bf16[1,129024]{1,0:T(2,128)(2,1)S(1)}, u32[]{:S(2)}, u32[]{:S(2)}) collective-permute-start(bf16[1,129024]{1,0:T(2,128)(2,1)S(1)} %get-tuple-element.24), channel_id=1, source_target_pairs={{0,3},{1,2},{2,1},{3,0},{4,7},{5,6},{6,5},{7,4},{8,11},{9,10},{10,... | collective-permute-start | bytes 774152 | tf_op jit(solution)/shard_map/ppermute | solution.py:18
  115.2 54.6 %collective-permute-start.3 = (bf16[1,129024]{1,0:T(2,128)(2,1)S(1)}, bf16[1,129024]{1,0:T(2,128)(2,1)S(1)}, u32[]{:S(2)}, u32[]{:S(2)}) collective-permute-start(bf16[1,129024]{1,0:T(2,128)(2,1)S(1)} %get-tuple-element.23), channel_id=1, source_target_pairs={{0,4},{1,5},{2,6},{3,7},{4,0},{5,1},{6,2},{7,3},{8,12},{9,13},{10,... | collective-permute-start | bytes 774152 | tf_op jit(solution)/shard_map/ppermute | solution.py:18
  117.0 64.9 %collective-permute-start.4 = (bf16[1,129024]{1,0:T(2,128)(2,1)S(1)}, bf16[1,129024]{1,0:T(2,128)(2,1)S(1)}, u32[]{:S(2)}, u32[]{:S(2)}) collective-permute-start(bf16[1,129024]{1,0:T(2,128)(2,1)S(1)} %get-tuple-element.22), channel_id=1, source_target_pairs={{0,5},{1,4},{2,7},{3,6},{4,1},{5,0},{6,3},{7,2},{8,13},{9,12},{10,... | collective-permute-start | bytes 774152 | tf_op jit(solution)/shard_map/ppermute | solution.py:18
  117.1 179.8 %copy-start.4 = (bf16[1,129024]{1,0:T(2,128)(2,1)}, bf16[1,129024]{1,0:T(2,128)(2,1)S(1)}, u32[]{:S(2)}) copy-start(bf16[1,129024]{1,0:T(2,128)(2,1)S(1)} %collective-permute-done) | copy-start | bytes 774148
  117.1 101.2 %collective-permute-start.5 = (bf16[1,129024]{1,0:T(2,128)(2,1)S(1)}, bf16[1,129024]{1,0:T(2,128)(2,1)S(1)}, u32[]{:S(2)}, u32[]{:S(2)}) collective-permute-start(bf16[1,129024]{1,0:T(2,128)(2,1)S(1)} %get-tuple-element.21), channel_id=1, source_target_pairs={{0,6},{1,7},{2,4},{3,5},{4,2},{5,3},{6,0},{7,1},{8,14},{9,15},{10,... | collective-permute-start | bytes 774152 | tf_op jit(solution)/shard_map/ppermute | solution.py:18
  136.3 160.6 %copy-start.5 = (bf16[1,129024]{1,0:T(2,128)(2,1)}, bf16[1,129024]{1,0:T(2,128)(2,1)S(1)}, u32[]{:S(2)}) copy-start(bf16[1,129024]{1,0:T(2,128)(2,1)S(1)} %collective-permute-done.1) | copy-start | bytes 774148
  136.3 92.0 %collective-permute-start.6 = (bf16[1,129024]{1,0:T(2,128)(2,1)S(1)}, bf16[1,129024]{1,0:T(2,128)(2,1)S(1)}, u32[]{:S(2)}, u32[]{:S(2)}) collective-permute-start(bf16[1,129024]{1,0:T(2,128)(2,1)S(1)} %get-tuple-element.20), channel_id=1, source_target_pairs={{0,7},{1,6},{2,5},{3,4},{4,3},{5,2},{6,1},{7,0},{8,15},{9,14},{10,... | collective-permute-start | bytes 774152 | tf_op jit(solution)/shard_map/ppermute | solution.py:18
  154.9 142.0 %copy-start.6 = (bf16[1,129024]{1,0:T(2,128)(2,1)}, bf16[1,129024]{1,0:T(2,128)(2,1)S(1)}, u32[]{:S(2)}) copy-start(bf16[1,129024]{1,0:T(2,128)(2,1)S(1)} %collective-permute-done.2) | copy-start | bytes 774148
  154.9 75.6 %collective-permute-start.7 = (bf16[1,129024]{1,0:T(2,128)(2,1)S(1)}, bf16[1,129024]{1,0:T(2,128)(2,1)S(1)}, u32[]{:S(2)}, u32[]{:S(2)}) collective-permute-start(bf16[1,129024]{1,0:T(2,128)(2,1)S(1)} %get-tuple-element.19), channel_id=1, source_target_pairs={{0,8},{1,9},{2,10},{3,11},{4,12},{5,13},{6,14},{7,15},{8,0},{9,1},... | collective-permute-start | bytes 774152 | tf_op jit(solution)/shard_map/ppermute | solution.py:18
  169.8 127.1 %copy-start.7 = (bf16[1,129024]{1,0:T(2,128)(2,1)}, bf16[1,129024]{1,0:T(2,128)(2,1)S(1)}, u32[]{:S(2)}) copy-start(bf16[1,129024]{1,0:T(2,128)(2,1)S(1)} %collective-permute-done.3) | copy-start | bytes 774148
  169.8 62.0 %collective-permute-start.8 = (bf16[1,129024]{1,0:T(2,128)(2,1)S(1)}, bf16[1,129024]{1,0:T(2,128)(2,1)S(1)}, u32[]{:S(2)}, u32[]{:S(2)}) collective-permute-start(bf16[1,129024]{1,0:T(2,128)(2,1)S(1)} %get-tuple-element.18), channel_id=1, source_target_pairs={{0,9},{1,8},{2,11},{3,10},{4,13},{5,12},{6,15},{7,14},{8,1},{9,0},... | collective-permute-start | bytes 774152 | tf_op jit(solution)/shard_map/ppermute | solution.py:18
  181.9 115.0 %copy-start.8 = (bf16[1,129024]{1,0:T(2,128)(2,1)}, bf16[1,129024]{1,0:T(2,128)(2,1)S(1)}, u32[]{:S(2)}) copy-start(bf16[1,129024]{1,0:T(2,128)(2,1)S(1)} %collective-permute-done.4) | copy-start | bytes 774148
  181.9 114.3 %collective-permute-start.9 = (bf16[1,129024]{1,0:T(2,128)(2,1)S(1)}, bf16[1,129024]{1,0:T(2,128)(2,1)S(1)}, u32[]{:S(2)}, u32[]{:S(2)}) collective-permute-start(bf16[1,129024]{1,0:T(2,128)(2,1)S(1)} %get-tuple-element.17), channel_id=1, source_target_pairs={{0,10},{1,11},{2,8},{3,9},{4,14},{5,15},{6,12},{7,13},{8,2},{9,3},... | collective-permute-start | bytes 774152 | tf_op jit(solution)/shard_map/ppermute | solution.py:18
  218.4 78.6 %copy-start.10 = (bf16[1,129024]{1,0:T(2,128)(2,1)}, bf16[1,129024]{1,0:T(2,128)(2,1)S(1)}, u32[]{:S(2)}) copy-start(bf16[1,129024]{1,0:T(2,128)(2,1)S(1)} %collective-permute-done.5) | copy-start | bytes 774148
  218.4 194.6 %collective-permute-start.10 = (bf16[1,129024]{1,0:T(2,128)(2,1)S(1)}, bf16[1,129024]{1,0:T(2,128)(2,1)}, u32[]{:S(2)}, u32[]{:S(2)}) collective-permute-start(bf16[1,129024]{1,0:T(2,128)(2,1)S(1)} %get-tuple-element.16), channel_id=1, source_target_pairs={{0,11},{1,10},{2,9},{3,8},{4,15},{5,14},{6,13},{7,12},{8,3},{9,2},... | collective-permute-start | bytes 774152 | tf_op jit(solution)/shard_map/ppermute | solution.py:18
  228.3 68.7 %copy-start.11 = (bf16[1,129024]{1,0:T(2,128)(2,1)}, bf16[1,129024]{1,0:T(2,128)(2,1)S(1)}, u32[]{:S(2)}) copy-start(bf16[1,129024]{1,0:T(2,128)(2,1)S(1)} %collective-permute-done.6) | copy-start | bytes 774148
  228.3 195.0 %collective-permute-start.11 = (bf16[1,129024]{1,0:T(2,128)(2,1)S(1)}, bf16[1,129024]{1,0:T(2,128)(2,1)}, u32[]{:S(2)}, u32[]{:S(2)}) collective-permute-start(bf16[1,129024]{1,0:T(2,128)(2,1)S(1)} %get-tuple-element.15), channel_id=1, source_target_pairs={{0,12},{1,13},{2,14},{3,15},{4,8},{5,9},{6,10},{7,11},{8,4},{9,5},... | collective-permute-start | bytes 774152 | tf_op jit(solution)/shard_map/ppermute | solution.py:18
  230.5 66.4 %copy-start.12 = (bf16[1,129024]{1,0:T(2,128)(2,1)}, bf16[1,129024]{1,0:T(2,128)(2,1)S(1)}, u32[]{:S(2)}) copy-start(bf16[1,129024]{1,0:T(2,128)(2,1)S(1)} %collective-permute-done.7) | copy-start | bytes 774148
  230.5 203.1 %collective-permute-start.12 = (bf16[1,129024]{1,0:T(2,128)(2,1)S(1)}, bf16[1,129024]{1,0:T(2,128)(2,1)}, u32[]{:S(2)}, u32[]{:S(2)}) collective-permute-start(bf16[1,129024]{1,0:T(2,128)(2,1)S(1)} %get-tuple-element.14), channel_id=1, source_target_pairs={{0,13},{1,12},{2,15},{3,14},{4,9},{5,8},{6,11},{7,10},{8,5},{9,4},... | collective-permute-start | bytes 774152 | tf_op jit(solution)/shard_map/ppermute | solution.py:18
  231.8 65.1 %copy-start.13 = (bf16[1,129024]{1,0:T(2,128)(2,1)}, bf16[1,129024]{1,0:T(2,128)(2,1)S(1)}, u32[]{:S(2)}) copy-start(bf16[1,129024]{1,0:T(2,128)(2,1)S(1)} %collective-permute-done.8) | copy-start | bytes 774148
  231.8 212.1 %collective-permute-start.13 = (bf16[1,129024]{1,0:T(2,128)(2,1)S(1)}, bf16[1,129024]{1,0:T(2,128)(2,1)}, u32[]{:S(2)}, u32[]{:S(2)}) collective-permute-start(bf16[1,129024]{1,0:T(2,128)(2,1)S(1)} %get-tuple-element.13), channel_id=1, source_target_pairs={{0,14},{1,15},{2,12},{3,13},{4,10},{5,11},{6,8},{7,9},{8,6},{9,7},... | collective-permute-start | bytes 774152 | tf_op jit(solution)/shard_map/ppermute | solution.py:18
  296.2 0.8 copy-start.14
  296.2 158.1 %collective-permute-start.14 = (bf16[1,129024]{1,0:T(2,128)(2,1)S(1)}, bf16[1,129024]{1,0:T(2,128)(2,1)}, u32[]{:S(2)}, u32[]{:S(2)}) collective-permute-start(bf16[1,129024]{1,0:T(2,128)(2,1)S(1)} %get-tuple-element.12), channel_id=1, source_target_pairs={{0,15},{1,14},{2,13},{3,12},{4,11},{5,10},{6,9},{7,8},{8,7},{9,6},... | collective-permute-start | bytes 774152 | tf_op jit(solution)/shard_map/ppermute | solution.py:18
  309.5 41.5 %copy-start.9 = (bf16[1,129024]{1,0:T(2,128)(2,1)S(1)}, bf16[1,129024]{1,0:T(2,128)(2,1)}, u32[]{:S(2)}) copy-start(bf16[1,129024]{1,0:T(2,128)(2,1)} %copy-done.8) | copy-start | bytes 774148
  361.3 41.4 %copy-start.15 = (bf16[1,129024]{1,0:T(2,128)(2,1)S(1)}, bf16[1,129024]{1,0:T(2,128)(2,1)}, u32[]{:S(2)}) copy-start(bf16[1,129024]{1,0:T(2,128)(2,1)} %copy-done.14) | copy-start | bytes 774148
  473.9 5.7 copy-start.2
  473.9 5.7 copy-start.24
  479.6 51.0 %copy-start.26 = (f32[576,512]{1,0:T(8,128)}, f32[576,512]{1,0:T(8,128)S(1)}, u32[]{:S(2)}) copy-start(f32[576,512]{1,0:T(8,128)S(1)} %fusion.2) | copy-start | bytes 3538948
  530.6 6.4 copy-start.23
  537.0 2.4 copy-start.25
  585.0 5.5 copy-start.3
  585.0 81.7 %all-to-all-start.2 = ((bf16[16,2,64512]{2,1,0:T(2,128)(2,1)}), bf16[16,2,64512]{2,1,0:T(2,128)(2,1)}, u32[]{:S(2)}, u32[]{:S(2)}) async-start(bf16[16,2,64512]{2,1,0:T(2,128)(2,1)} %reshape.140), calls=%async_computation.2 | async-start | bytes 8257536 | tf_op jit(solution)/shard_map/all_to_all | solution.py:110
  590.3 127.7 %reduce-scatter.5.cloned.1.call-start = ((), (), s32[]{:S(2)}) async-start(), calls=%async_computation.6 | async-start | bytes 4128768 | tf_op jit(solution)/shard_map/reduce_scatter | solution.py:103
  601.0 145.8 %reduce-scatter.3.cloned.1.call-start = ((), (), s32[]{:S(2)}) async-start(), calls=%async_computation.5 | async-start | bytes 688128 | tf_op jit(solution)/shard_map/reduce_scatter | solution.py:120
  705.0 9.1 %copy-start.18 = (s32[576]{0:T(1024)S(1)}, s32[576]{0:T(1024)}, u32[]{:S(2)}) copy-start(s32[576]{0:T(1024)} %copy-done.17) | copy-start | bytes 6916
  705.0 9.1 %copy-start.20 = (pred[576]{0:T(1024)(128)(4,1)S(1)}, pred[576]{0:T(1024)(128)(4,1)}, u32[]{:S(2)}) copy-start(pred[576]{0:T(1024)(128)(4,1)} %copy-done.19) | copy-start | bytes 1732
  705.0 41.8 %copy-start.1 = (bf16[64,3584]{1,0:T(8,128)(2,1)S(1)}, bf16[64,3584]{1,0:T(8,128)(2,1)}, u32[]{:S(2)}) copy-start(bf16[64,3584]{1,0:T(8,128)(2,1)} %param.8) | copy-start | bytes 1376260
Sparse Core Ops, SparseCore 0:
  601.1 40.3 reduce-scatter.4
  718.1 28.6 reduce-scatter.2
